TPU v7x, 256 devices: a whole 4x4x8 slice. The times are simulated.
256 devices in a mesh: ctx: 128 (over z, x_lo, y, core), head: 2 (over x_hi).
Axes of the slice: x: 4 (x_hi: 2, x_lo: 2; x = x_hi * 2 + x_lo), y: 4, z: 8, core: 2. Of those that a mesh axis runs over, the one named last changes fastest.
Arguments:
- queries: bfloat16 [65536, 2048], P('ctx', 'head'), may hold values from -13 to 13, as said below
- keys: bfloat16 [65536, 512], P('ctx', 'head'), may hold values from -13 to 13
- values: bfloat16 [65536, 512], P('ctx', 'head'), may hold values from -24 to 24
- positions: int32 [65536], P('ctx'), may hold values from 0 to 32767, as said below
- out_weight: bfloat16 [2048, 4096], P(None, 'head'), may hold values from -0.125 to 0.125
Outputs:
- mixed: bfloat16 [65536, 4096], P('ctx', 'head')
Inputs may be any that keep to these rules, and one draw needn't show every extreme that they name: queries, keys: every entry lies in the stated range. positions[r] is 0 where the token at sequence position g(r) begins a document and one more than the position of the token at g(r) - 1 otherwise; documents begin at sequence positions 0 and 32768 and possibly elsewhere in the first half; the second half is one document.
All inputs are finite; a program needn't handle non-finite values.
Results may differ from a plain program's by a relative error of at most 0.012.
The roundings to bfloat16 on the way count: a program that leaves them out, or rounds other values in their place, can miss the bound.
Values may be sent and summed in bfloat16 or wider, within the bound.
A program may use at most 128 MiB of HBM per device.

v0:
```python
import math
import jax
import jax.numpy as jnp
import numpy as np
from jax import lax
from jax.sharding import PartitionSpec as P

HEAD_SIZE = 128
STEPS = 4
neg_large = -1e30


def passed_along(value, axis, steps):
    count = lax.axis_size(axis)
    pairs = [(source, (source + steps) % count) for source in range(count)]
    return lax.ppermute(value, axis, pairs)


def rotate(block, positions, width):
    halfway = width // 2
    table = np.power(500000.0, -2.0 * np.arange(halfway) / width).astype(np.float32)
    angle = positions.astype(jnp.float32)[:, None] * jnp.asarray(table, dtype=jnp.float32)[None, :]
    cosine = jnp.cos(angle)[:, None, :]
    sinus = jnp.sin(angle)[:, None, :]
    number = block.shape[0]
    groups = block.shape[1] // width
    split_up = block.astype(jnp.float32).reshape(number, groups, width)
    leading = split_up[:, :, :halfway]
    trailing = split_up[:, :, halfway:]
    turned = jnp.concatenate(
        [leading * cosine - trailing * sinus, trailing * cosine + leading * sinus], axis=2
    )
    return turned.reshape(number, groups * width).astype(jnp.bfloat16)


def make_index(block_number, cycle_size, number):
    halfway = number // 2
    within = jnp.arange(number, dtype=jnp.int32)
    early = block_number * halfway + within
    late = (2 * cycle_size - 1 - block_number) * halfway + within - halfway
    return jnp.where(within < halfway, early, late)


def attend(
    state, query_part, query_index, query_start, key_part, value_part, key_index, query_group
):
    maxima, totals, sums = state
    number = query_part.shape[0]
    shaped_query = query_part.reshape(number, -1, query_group, HEAD_SIZE)
    shaped_key = key_part.reshape(key_part.shape[0], -1, HEAD_SIZE)
    shaped_value = value_part.reshape(value_part.shape[0], -1, HEAD_SIZE)
    scores = jnp.einsum(
        "qhgd,khd->hgqk", shaped_query, shaped_key, preferred_element_type=jnp.float32
    ) * (1.0 / math.sqrt(HEAD_SIZE))
    allowed = (key_index[None, :] <= query_index[:, None]) & (
        key_index[None, :] >= query_start[:, None]
    )
    scores = jnp.where(allowed, scores, neg_large)
    updated = jnp.maximum(maxima, jnp.max(scores, axis=3))
    weights = jnp.where(allowed, jnp.exp(scores - updated[..., None]), 0.0)
    factor = jnp.exp(maxima - updated)
    totals = totals * factor + jnp.sum(weights, axis=3)
    added = jnp.einsum(
        "hgqk,khd->qhgd",
        weights.astype(jnp.bfloat16),
        shaped_value,
        preferred_element_type=jnp.float32,
    )
    sums = sums * jnp.transpose(factor, (2, 0, 1))[..., None] + added
    return (updated, totals, sums)


def attend_rows(
    state, lower, upper, q_rot, index_of, doc_start, key_part, value_part, key_index, query_group
):
    maxima, totals, sums = state
    sliced = (maxima, totals, sums)
    new_max, new_total, new_sums = attend(
        sliced, q_rot, index_of, doc_start, key_part, value_part, key_index, query_group
    )
    return (
        maxima.at[:, :, lower:upper].set(new_max),
        totals.at[:, :, lower:upper].set(new_total),
        sums.at[lower:upper].set(new_sums),
    )


def shards(queries, keys, values, positions, out_weight):
    number = queries.shape[0]
    cycle_size = lax.axis_size("ctx")
    rank = lax.axis_index("ctx")
    kv_local = keys.shape[1] // HEAD_SIZE
    query_group = queries.shape[1] // keys.shape[1]
    index_of = make_index(rank, cycle_size, number)
    doc_start = index_of - positions
    q_rot = rotate(queries, positions, HEAD_SIZE)
    rotary_keys = rotate(keys, positions, HEAD_SIZE)
    state = (
        jnp.full((kv_local, query_group, number), neg_large, jnp.float32),
        jnp.zeros((kv_local, query_group, number), jnp.float32),
        jnp.zeros((number, kv_local, query_group, HEAD_SIZE), jnp.float32),
    )
    state = attend_rows(
        state, 0, number, q_rot, index_of, doc_start, rotary_keys, values, index_of, query_group
    )
    travel = (rotary_keys, values)
    for step in range(1, STEPS):
        travel = passed_along((travel[0], travel[1]), "ctx", 1)
        key_row_slice, value_rows = travel
        source = (rank - step) % cycle_size
        key_index = make_index(source, cycle_size, number)
        state = attend_rows(
            state,
            0,
            number,
            q_rot,
            index_of,
            doc_start,
            key_row_slice,
            value_rows,
            key_index,
            query_group,
        )
    maxima, totals, sums = state
    attended = (
        (sums / jnp.transpose(totals, (2, 0, 1))[..., None])
        .reshape(number, kv_local * query_group * HEAD_SIZE)
        .astype(jnp.bfloat16)
    )
    mixed = jnp.dot(
        lax.all_gather(attended, "head", axis=1, tiled=True),
        out_weight,
        preferred_element_type=jnp.float32,
    )
    return mixed.astype(jnp.bfloat16)


def solution(mesh):
    in_specs = (P("ctx", "head"), P("ctx", "head"), P("ctx", "head"), P("ctx"), P(None, "head"))
    out_specs = P("ctx", "head")
    return jax.shard_map(shards, mesh=mesh, in_specs=in_specs, out_specs=out_specs, check_vma=False)
```

profile of v0, /device:TPU:1, one launch (start us, length us, event | category | flops | bytes accessed | tf_op | source)
XLA Modules:
  0.0 138.5 jit_solution(5916004114600088739)
XLA Ops:
  6.5 0.0 copy-start.1
  6.5 0.0 all-gather.2.cloned.1.call-start
  6.5 1.2 copy.18
  7.7 0.1 fusion.58
  7.8 0.2 copy.54
  8.0 0.2 copy.55
  8.2 0.8 fusion.40
  9.0 1.6 %multiply_cosine_fusion = (f32[512,64]{1,0:T(8,128)S(1)}, f32[512,64]{1,0:T(8,128)S(1)}) fusion(f32[64]{0:T(128)} %constant.404.clone, f32[512]{0:T(512)S(1)} %get-tuple-element.249), kind=kLoop, calls=%fused_computation.50 | loop fusion | flops 32768 | bytes 264448 | tf_op jit(solution)/shard_map/cos | solution.py:23
  10.6 0.1 multiply_subtract_fusion
  10.8 0.1 maximum_convert_fusion
  10.9 0.1 copy.25
  11.1 2.8 %collective-permute-start = (bf16[512,256]{0,1:T(8,128)(2,1)S(1)}, bf16[512,256]{0,1:T(8,128)(2,1)}, u32[]{:S(2)}, u32[]{:S(2)}) collective-permute-start(bf16[512,256]{0,1:T(8,128)(2,1)S(1)} %bitcast.211), channel_id=1, source_target_pairs={{0,2},{2,4},{4,6},{6,8},{8,10},{10,12},{12,14},{14,16},{16,18},{18... | collective-permute-start | bytes 786440 | tf_op jit(solution)/shard_map/ppermute | solution.py:16
  13.8 0.1 collective-permute-start.1
  13.9 1.1 copy.47
  15.1 0.0 copy-done.1
  15.1 0.2 convert_bitcast_fusion
  15.3 0.5 copy.58
  15.8 0.7 fusion.57
  16.5 0.8 subtract_convert_fusion
  17.3 0.6 pad_maximum_fusion
  17.9 1.0 compare_and_fusion.3
  18.9 4.7 %fusion = (f32[2,4,512]{2,1,0:T(4,128)S(1)}, f32[2,512,512,4]{2,1,3,0:T(8,128)}) fusion(pred[512,512]{0,1:T(8,128)(4,1)S(1)} %get-tuple-element.242, bf16[512,2,4,128]{3,0,2,1:T(8,128)(2,1)S(1)} %bitcast.202, bf16[512,2,128]{2,0,1:T(8,128)(2,1)S(1)} %maximum_convert_fusion), kind=kOutput, calls=%fused_computation.8 | convolution fusion | flops 543158272 | bytes 9977856 | tf_op jit(solution)/shard_map/qhgd,khd->hgqk/dot_general | solution.py:52
  23.6 0.0 collective-permute-done.1
  23.6 0.9 copy.27
  24.5 1.6 %collective-permute-start.3 = (bf16[512,256]{1,0:T(8,128)(2,1)S(1)}, bf16[512,256]{1,0:T(8,128)(2,1)S(1)}, u32[]{:S(2)}, u32[]{:S(2)}) collective-permute-start(bf16[512,256]{1,0:T(8,128)(2,1)S(1)} %collective-permute-done.1), channel_id=1, source_target_pairs={{0,2},{2,4},{4,6},{6,8},{8,10},{10,12},{12,14},{14,16},{16,18},{18... | collective-permute-start | bytes 786440 | tf_op jit(solution)/shard_map/ppermute | solution.py:16
  26.1 0.0 collective-permute-done
  26.1 0.1 collective-permute-start.2
  26.2 5.9 %fusion.1 = (f32[2,4,512]{2,1,0:T(4,128)S(1)}, f32[2,512,512,4]{2,1,3,0:T(8,128)}) fusion(pred[512,512]{0,1:T(8,128)(4,1)S(1)} %get-tuple-element.243, bf16[512,2,128,1]{0,2,3,1:T(8,128)(2,1)} %bitcast.45, bf16[512,2,4,128]{3,0,2,1:T(8,128)(2,1)S(1)} %bitcast.203), kind=kOutput, calls=%fused_computation.9 | convolution fusion | flops 543158272 | bytes 9977856 | tf_op jit(solution)/shard_map/qhgd,khd->hgqk/dot_general | solution.py:52
  32.0 0.0 collective-permute-done.3
  32.1 0.8 copy.30
  32.9 1.2 collective-permute-start.5
  34.1 0.0 collective-permute-done.2
  34.1 0.5 collective-permute-start.4
  34.7 0.0 slice-start
  34.7 2.0 %fusion.2 = (f32[2,4,512]{2,1,0:T(4,128)S(1)}, f32[2,512,512,4]{2,1,3,0:T(8,128)S(1)}) fusion(pred[512,512]{0,1:T(8,128)(4,1)S(1)} %get-tuple-element.244, bf16[512,2,128,1]{0,2,3,1:T(8,128)(2,1)S(1)} %bitcast.209, bf16[512,2,4,128]{3,0,2,1:T(8,128)(2,1)S(1)} %bitcast.204), kind=kOutput, calls=%fused_computation.10 | convolution fusion | flops 543158272 | bytes 9977856 | tf_op jit(solution)/shard_map/qhgd,khd->hgqk/dot_general | solution.py:52
  36.7 6.2 %collective-permute-done.4 = bf16[512,256]{0,1:T(8,128)(2,1)S(1)} collective-permute-done((bf16[512,256]{0,1:T(8,128)(2,1)S(1)}, bf16[512,256]{0,1:T(8,128)(2,1)S(1)}, u32[]{:S(2)}, u32[]{:S(2)}) %collective-permute-start.4) | collective-permute-done | bytes 262176 | tf_op jit(solution)/shard_map/ppermute | solution.py:16
  42.9 0.0 slice-start.1
  42.9 2.0 %fusion.3 = (f32[2,4,512]{2,1,0:T(4,128)S(1)}, f32[2,512,512,4]{2,1,3,0:T(8,128)S(1)}) fusion(pred[512,512]{0,1:T(8,128)(4,1)S(1)} %get-tuple-element.245, bf16[512,2,128,1]{0,2,3,1:T(8,128)(2,1)S(1)} %bitcast.210, bf16[512,2,4,128]{3,0,2,1:T(8,128)(2,1)S(1)} %bitcast.205), kind=kOutput, calls=%fused_computation.11 | convolution fusion | flops 543158272 | bytes 9977856 | tf_op jit(solution)/shard_map/qhgd,khd->hgqk/dot_general | solution.py:52
  44.9 0.0 copy-start
  45.0 0.0 slice-done
  45.0 0.1 slice-done.1
  45.1 2.0 %fusion.4 = f32[2,4,512]{2,1,0:T(4,128)S(1)} fusion(f32[2,512,512,4]{2,1,3,0:T(8,128)S(1)} %bitcast.199, f32[2,4,512]{2,1,0:T(4,128)S(1)} %get-tuple-element.241, pred[512,512]{0,1:T(8,128)(4,1)S(1)} %get-tuple-element.242), kind=kLoop, calls=%fused_computation.12 | loop fusion | flops 10481664 | bytes 8683520 | tf_op jit(solution)/shard_map/reduce_sum | solution.py:62
  47.1 0.0 slice-start.2
  47.1 0.0 slice-start.3
  47.1 3.8 %fusion.18 = f32[2,4,512,128]{2,3,1,0:T(8,128)} fusion(bf16[512,2,128,1]{0,2,3,1:T(8,128)(2,1)S(1)} %bitcast.212, f32[2,512,512,4]{2,1,3,0:T(8,128)S(1)} %bitcast.199, f32[2,4,512]{2,1,0:T(4,128)S(1)} %get-tuple-element.241, pred[512,512]{0,1:T(8,128)(4,1)S(1)} %get-tuple-element.242), kind=kOutput, calls=%fused_computation.23 | convolution fusion | flops 547356672 | bytes 11026432 | tf_op jit(solution)/shard_map/hgqk,khd->qhgd/dot_general | solution.py:63
  51.0 0.0 copy-start.2
  51.0 0.0 slice-done.2
  51.0 1.0 slice-done.3
  52.0 2.0 %fusion.6 = f32[2,4,512]{2,1,0:T(4,128)S(1)} fusion(f32[2,512,512,4]{2,1,3,0:T(8,128)S(1)} %bitcast.201, f32[2,4,512]{2,1,0:T(4,128)S(1)} %get-tuple-element.230, pred[512,512]{0,1:T(8,128)(4,1)S(1)} %get-tuple-element.243), kind=kLoop, calls=%fused_computation.14 | loop fusion | flops 10481664 | bytes 8683520 | tf_op jit(solution)/shard_map/reduce_sum | solution.py:62
  54.0 0.0 copy-done.2
  54.0 3.9 %fusion.16 = f32[2,4,512,128]{2,3,1,0:T(8,128)} fusion(bf16[512,2,128,1]{0,2,3,1:T(8,128)(2,1)S(1)} %bitcast.213, f32[2,512,512,4]{2,1,3,0:T(8,128)S(1)} %bitcast.201, f32[2,4,512]{2,1,0:T(4,128)S(1)} %get-tuple-element.230, pred[512,512]{0,1:T(8,128)(4,1)S(1)} %get-tuple-element.243), kind=kOutput, calls=%fused_computation.22 | convolution fusion | flops 547356672 | bytes 11026432 | tf_op jit(solution)/shard_map/hgqk,khd->qhgd/dot_general | solution.py:63
  57.9 0.0 copy-start.3
  57.9 2.0 %fusion.8 = f32[2,4,512]{2,1,0:T(4,128)S(1)} fusion(f32[2,512,512,4]{2,1,3,0:T(8,128)S(1)} %get-tuple-element.253, f32[2,4,512]{2,1,0:T(4,128)S(1)} %get-tuple-element.229, pred[512,512]{0,1:T(8,128)(4,1)S(1)} %get-tuple-element.244), kind=kLoop, calls=%fused_computation.16 | loop fusion | flops 10481664 | bytes 8683520 | tf_op jit(solution)/shard_map/reduce_sum | solution.py:62
  59.9 0.0 copy-done.3
  59.9 3.8 %fusion.14 = f32[2,4,512,128]{2,3,1,0:T(8,128)} fusion(bf16[512,2,128,1]{0,2,3,1:T(8,128)(2,1)S(1)} %bitcast.214, f32[2,512,512,4]{2,1,3,0:T(8,128)S(1)} %get-tuple-element.253, f32[2,4,512]{2,1,0:T(4,128)S(1)} %get-tuple-element.229, pred[512,512]{0,1:T(8,128)(4,1)S(1)} %get-tuple-element.244), kind=kOutput, calls=%fused_computation.21 | convolution fusion | flops 547356672 | bytes 11026432 | tf_op jit(solution)/shard_map/hgqk,khd->qhgd/dot_general | solution.py:63
  63.7 0.0 copy-done
  63.7 2.0 %fusion.10 = f32[2,4,512]{2,1,0:T(4,128)S(1)} fusion(f32[2,512,512,4]{2,1,3,0:T(8,128)S(1)} %get-tuple-element.251, f32[2,4,512]{2,1,0:T(4,128)S(1)} %get-tuple-element.228, pred[512,512]{0,1:T(8,128)(4,1)S(1)} %get-tuple-element.245), kind=kLoop, calls=%fused_computation.18 | loop fusion | flops 10481664 | bytes 8683520 | tf_op jit(solution)/shard_map/reduce_sum | solution.py:62
  65.8 0.0 collective-permute-done.5
  65.8 0.1 copy.33
  66.0 9.1 %fusion.25 = bf16[512,2,4,128]{0,3,2,1:T(8,128)(2,1)} fusion(f32[2,4,512,128]{2,3,1,0:T(8,128)} %fusion.14, f32[2,4,512,128]{2,3,1,0:T(8,128)} %fusion.16, f32[2,4,512,128]{2,3,1,0:T(8,128)} %fusion.18, bf16[512,2,128,1]{0,2,3,1:T(8,128)(2,1)S(1)} %bitcast.215, f32[2,512,512,4]{2,1,3,0:T(8,128)} %copy-done, f32[2,4,512]{2,1,0:T(4,128)S(1)} %get-tuple-element.228, ...), kind=kOutput, calls=%fused_computation.31 | convolution fusion | flops 552075264 | bytes 16351232 | tf_op jit(solution)/shard_map/hgqk,khd->qhgd/dot_general | solution.py:63
  75.1 0.0 all-gather.2.cloned.1.call-update
  75.1 46.6 %all-gather.2.cloned.1.call-done = bf16[512,2048]{0,1:T(8,128)(2,1)} async-done(((bf16[512,1024]{0,1:T(8,128)(2,1)}), bf16[512,2048]{0,1:T(8,128)(2,1)}) %all-gather.2.cloned.1.call-update) | async-done | bytes 2097168 | tf_op jit(solution)/shard_map/all_gather | solution.py:131
  121.7 9.9 %convolution_convert_fusion = bf16[512,2048]{1,0:T(8,128)(2,1)} fusion(bf16[512,2048]{0,1:T(8,128)(2,1)} %all-gather.2.cloned.1.call-done, bf16[2048,2048]{1,0:T(8,128)(2,1)} %param.55), kind=kOutput, calls=%fused_computation.28 | convolution fusion | flops 4296015872 | bytes 12582912 | tf_op jit(solution)/shard_map/dot_general | solution.py:130
  (6 shorter events, 0.1 us)
Async XLA Ops:
  6.5 8.5 %copy-start.1 = (bf16[512,1024]{1,0:T(8,128)(2,1)S(1)}, bf16[512,1024]{1,0:T(8,128)(2,1)}, u32[]{:S(2)}) copy-start(bf16[512,1024]{1,0:T(8,128)(2,1)} %param.51) | copy-start | bytes 3145732
  6.5 115.2 %all-gather.2.cloned.1.call-start = ((), (), s32[]{:S(2)}) async-start(), calls=%async_computation | async-start | bytes 3145728 | tf_op jit(solution)/shard_map/all_gather | solution.py:131
  11.1 15.0 %collective-permute-start = (bf16[512,256]{0,1:T(8,128)(2,1)S(1)}, bf16[512,256]{0,1:T(8,128)(2,1)}, u32[]{:S(2)}, u32[]{:S(2)}) collective-permute-start(bf16[512,256]{0,1:T(8,128)(2,1)S(1)} %bitcast.211), channel_id=1, source_target_pairs={{0,2},{2,4},{4,6},{6,8},{8,10},{10,12},{12,14},{14,16},{16,18},{18... | collective-permute-start | bytes 786440 | tf_op jit(solution)/shard_map/ppermute | solution.py:16
  13.8 9.8 %collective-permute-start.1 = (bf16[512,256]{1,0:T(8,128)(2,1)}, bf16[512,256]{1,0:T(8,128)(2,1)S(1)}, u32[]{:S(2)}, u32[]{:S(2)}) collective-permute-start(bf16[512,256]{1,0:T(8,128)(2,1)} %param.53), channel_id=1, source_target_pairs={{0,2},{2,4},{4,6},{6,8},{8,10},{10,12},{12,14},{14,16},{16,18},{18... | collective-permute-start | bytes 786440 | tf_op jit(solution)/shard_map/ppermute | solution.py:16
  24.5 7.6 %collective-permute-start.3 = (bf16[512,256]{1,0:T(8,128)(2,1)S(1)}, bf16[512,256]{1,0:T(8,128)(2,1)S(1)}, u32[]{:S(2)}, u32[]{:S(2)}) collective-permute-start(bf16[512,256]{1,0:T(8,128)(2,1)S(1)} %collective-permute-done.1), channel_id=1, source_target_pairs={{0,2},{2,4},{4,6},{6,8},{8,10},{10,12},{12,14},{14,16},{16,18},{18... | collective-permute-start | bytes 786440 | tf_op jit(solution)/shard_map/ppermute | solution.py:16
  26.1 8.1 %collective-permute-start.2 = (bf16[512,256]{0,1:T(8,128)(2,1)}, bf16[512,256]{0,1:T(8,128)(2,1)S(1)}, u32[]{:S(2)}, u32[]{:S(2)}) collective-permute-start(bf16[512,256]{0,1:T(8,128)(2,1)} %collective-permute-done), channel_id=1, source_target_pairs={{0,2},{2,4},{4,6},{6,8},{8,10},{10,12},{12,14},{14,16},{16,18},{18... | collective-permute-start | bytes 786440 | tf_op jit(solution)/shard_map/ppermute | solution.py:16
  32.9 32.9 %collective-permute-start.5 = (bf16[512,256]{1,0:T(8,128)(2,1)S(1)}, bf16[512,256]{1,0:T(8,128)(2,1)S(1)}, u32[]{:S(2)}, u32[]{:S(2)}) collective-permute-start(bf16[512,256]{1,0:T(8,128)(2,1)S(1)} %collective-permute-done.3), channel_id=1, source_target_pairs={{0,2},{2,4},{4,6},{6,8},{8,10},{10,12},{12,14},{14,16},{16,18},{18... | collective-permute-start | bytes 786440 | tf_op jit(solution)/shard_map/ppermute | solution.py:16
  34.1 8.8 %collective-permute-start.4 = (bf16[512,256]{0,1:T(8,128)(2,1)S(1)}, bf16[512,256]{0,1:T(8,128)(2,1)S(1)}, u32[]{:S(2)}, u32[]{:S(2)}) collective-permute-start(bf16[512,256]{0,1:T(8,128)(2,1)S(1)} %collective-permute-done.2), channel_id=1, source_target_pairs={{0,2},{2,4},{4,6},{6,8},{8,10},{10,12},{12,14},{14,16},{16,18},{18... | collective-permute-start | bytes 786440 | tf_op jit(solution)/shard_map/ppermute | solution.py:16
  34.7 10.3 %slice-start = ((s8[8388608]{0:T(1024)(128)(4,1)}), s8[4194304]{0:T(1024)(128)(4,1)S(1)}, s32[]{:S(2)}) async-start(s8[8388608]{0:T(1024)(128)(4,1)} %bitcast.198), calls=%async_computation.1 | async-start | bytes 8388608
  42.9 2.2 %slice-start.1 = ((s8[8388608]{0:T(1024)(128)(4,1)}), s8[4194304]{0:T(1024)(128)(4,1)S(1)}, s32[]{:S(2)}) async-start(s8[8388608]{0:T(1024)(128)(4,1)} %bitcast.198), calls=%async_computation.2 | async-start | bytes 8388608
  44.9 18.8 %copy-start = (f32[2,512,512,4]{2,1,3,0:T(8,128)}, f32[2,512,512,4]{2,1,3,0:T(8,128)S(1)}, u32[]{:S(2)}) copy-start(f32[2,512,512,4]{2,1,3,0:T(8,128)S(1)} %get-tuple-element.251) | copy-start | bytes 25165828
  47.1 3.8 %slice-start.2 = ((s8[8388608]{0:T(1024)(128)(4,1)}), s8[4194304]{0:T(1024)(128)(4,1)S(1)}, s32[]{:S(2)}) async-start(s8[8388608]{0:T(1024)(128)(4,1)} %bitcast.200), calls=%async_computation.3 | async-start | bytes 8388608
  47.1 4.9 %slice-start.3 = ((s8[8388608]{0:T(1024)(128)(4,1)}), s8[4194304]{0:T(1024)(128)(4,1)S(1)}, s32[]{:S(2)}) async-start(s8[8388608]{0:T(1024)(128)(4,1)} %bitcast.200), calls=%async_computation.4 | async-start | bytes 8388608
  51.0 3.1 %copy-start.2 = (bf16[512,256]{0,1:T(8,128)(2,1)S(1)}, bf16[512,256]{0,1:T(8,128)(2,1)}, u32[]{:S(2)}) copy-start(bf16[512,256]{0,1:T(8,128)(2,1)} %copy.27) | copy-start | bytes 786436
  57.9 2.0 %copy-start.3 = (bf16[512,256]{0,1:T(8,128)(2,1)S(1)}, bf16[512,256]{0,1:T(8,128)(2,1)}, u32[]{:S(2)}) copy-start(bf16[512,256]{0,1:T(8,128)(2,1)} %copy.30) | copy-start | bytes 786436
Sparse Core Ops, SparseCore 0:
  75.2 46.4 all-gather.1
where the time goes:
time: 139 us; the launch traced here: 138 us
  waiting for transfers between devices  52.9 us (38%)
  matrix products  45.1 us (32%)
  between operations  13.7 us (10%)
  other arithmetic  13.5 us (10%)
  local copies, waits for them, and re-layouts  7.03 us (5%)
  starting transfers between devices  6.31 us (5%)
    all_gather x1, waiting for transfers between devices, shards(): lax.all_gather(attended, 'head', axis=1, tiled=True)  46.6 us
    dot_general x4, matrix products, attend(): jnp.einsum('hgqk,khd->qhgd', weights.astype(jnp.bfloat16), shaped_value,...  20.6 us
    dot_general x4, matrix products, attend(): jnp.einsum('qhgd,khd->hgqk', shaped_query, shaped_key, preferred_element_...  14.6 us
    dot_general x1, matrix products, shards(): jnp.dot(lax.all_gather(attended, 'head', axis=1, tiled=True), out_weight,...  9.9 us
    reduce_sum x4, other arithmetic, attend(): totals = totals * factor + jnp.sum(weights, axis=3)  8.1 us
    ppermute x6, starting transfers between devices, passed_along(): return lax.ppermute(value, axis, pairs)  6.31 us
    ppermute x6, waiting for transfers between devices, passed_along(): return lax.ppermute(value, axis, pairs)  6.22 us
    unnamed x20, local copies, waits for them, and re-layouts  3.2 us
  transfers between devices with their start and end apart: 7, of which 2 were waited for; matrix products, arithmetic and copies ran while one was open for 30% of the time, Pallas kernels for 0%

commit v1 on v0

--- a/solution.py
+++ b/solution.py
@@ -128,7 +128,9 @@
         .astype(jnp.bfloat16)
     )
     mixed = jnp.dot(
-        lax.all_gather(attended, "head", axis=1, tiled=True),
+        jnp.concatenate(
+            lax.all_to_all(jnp.stack([attended] * lax.axis_size("head")), "head", 0, 0), axis=1
+        ),
         out_weight,
         preferred_element_type=jnp.float32,
     )

time: 139 us -> 108 us (0.78)
  the two profiles are of different devices: /device:TPU:1 before, /device:TPU:123 now
where the time goes in v1:
time: 108 us
  matrix products  43.3 us (40%)
  blocking collectives  29.3 us (27%)
  other arithmetic  13.7 us (13%)
  starting transfers between devices  12.3 us (11%)
  local copies, waits for them, and re-layouts  7.02 us (6%)
  waiting for transfers between devices  2.14 us (2%)
    all_to_all x1, blocking collectives, shards(): lax.all_to_all(jnp.stack([attended] * lax.axis_size('head')), 'head', 0, 0)  29.3 us
    dot_general x4, matrix products, attend(): jnp.einsum('hgqk,khd->qhgd', weights.astype(jnp.bfloat16), shaped_value,...  19.6 us
    dot_general x4, matrix products, attend(): jnp.einsum('qhgd,khd->hgqk', shaped_query, shaped_key, preferred_element_...  14.6 us
    ppermute x6, starting transfers between devices, passed_along(): return lax.ppermute(value, axis, pairs)  12.3 us
    dot_general x1, matrix products, shards(): jnp.dot(jnp.concatenate(lax.all_to_all(jnp.stack([attended] * lax.axis_si...  9.1 us
    reduce_sum x4, other arithmetic, attend(): totals = totals * factor + jnp.sum(weights, axis=3)  8.1 us
    unnamed x20, local copies, waits for them, and re-layouts  3.19 us
  transfers between devices with their start and end apart: 6, of which 1 were waited for; matrix products, arithmetic and copies ran while one was open for 38% of the time, Pallas kernels for 0%

profile of v1, /device:TPU:123, one launch (start us, length us, event | category | flops | bytes accessed | tf_op | source)
XLA Modules:
  0.0 108.1 jit_solution(17598973808371512161)
XLA Ops:
  0.0 0.0 copy-start.1
  0.0 1.2 %copy.18 = bf16[512,256]{0,1:T(8,128)(2,1)S(1)} copy(bf16[512,256]{1,0:T(8,128)(2,1)} %param.52) | data formatting | bytes 524288 | tf_op args[1]
  1.2 0.1 fusion.58
  1.2 0.2 copy.54
  1.4 0.2 copy.55
  1.7 0.8 fusion.40
  2.4 1.6 %multiply_cosine_fusion = (f32[512,64]{1,0:T(8,128)S(1)}, f32[512,64]{1,0:T(8,128)S(1)}) fusion(f32[64]{0:T(128)} %constant.404.clone, f32[512]{0:T(512)S(1)} %get-tuple-element.249), kind=kLoop, calls=%fused_computation.51 | loop fusion | flops 32768 | bytes 264448 | tf_op jit(solution)/shard_map/cos | solution.py:23
  4.1 0.1 multiply_subtract_fusion
  4.2 0.1 maximum_convert_fusion
  4.4 0.1 copy.25
  4.5 3.1 %collective-permute-start = (bf16[512,256]{0,1:T(8,128)(2,1)S(1)}, bf16[512,256]{0,1:T(8,128)(2,1)}, u32[]{:S(2)}, u32[]{:S(2)}) collective-permute-start(bf16[512,256]{0,1:T(8,128)(2,1)S(1)} %bitcast.215), channel_id=1, source_target_pairs={{0,2},{2,4},{4,6},{6,8},{8,10},{10,12},{12,14},{14,16},{16,18},{18... | collective-permute-start | bytes 786440 | tf_op jit(solution)/shard_map/ppermute | solution.py:16
  7.6 0.1 collective-permute-start.1
  7.7 1.1 %copy.47 = bf16[512,256]{0,1:T(8,128)(2,1)S(1)} copy(bf16[512,256]{1,0:T(8,128)(2,1)} %param.53) | data formatting | bytes 524288 | tf_op jit(solution)/shard_map/reshape | solution.py:51
  8.9 0.0 copy-done.1
  8.9 0.2 convert_bitcast_fusion
  9.1 0.5 copy.58
  9.6 0.7 fusion.57
  10.3 0.8 subtract_convert_fusion
  11.1 0.6 pad_maximum_fusion.1
  11.7 1.0 compare_and_fusion.3
  12.8 4.7 %fusion = (f32[2,4,512]{2,1,0:T(4,128)S(1)}, f32[2,512,512,4]{2,1,3,0:T(8,128)}) fusion(pred[512,512]{0,1:T(8,128)(4,1)S(1)} %get-tuple-element.242, bf16[512,2,4,128]{3,0,2,1:T(8,128)(2,1)S(1)} %bitcast.205, bf16[512,2,128]{2,0,1:T(8,128)(2,1)S(1)} %maximum_convert_fusion), kind=kOutput, calls=%fused_computation.8 | convolution fusion | flops 543158272 | bytes 9977856 | tf_op jit(solution)/shard_map/qhgd,khd->hgqk/dot_general | solution.py:52
  17.5 0.0 collective-permute-done.1
  17.5 0.9 copy.27
  18.3 3.0 %collective-permute-start.3 = (bf16[512,256]{1,0:T(8,128)(2,1)S(1)}, bf16[512,256]{1,0:T(8,128)(2,1)S(1)}, u32[]{:S(2)}, u32[]{:S(2)}) collective-permute-start(bf16[512,256]{1,0:T(8,128)(2,1)S(1)} %collective-permute-done.1), channel_id=1, source_target_pairs={{0,2},{2,4},{4,6},{6,8},{8,10},{10,12},{12,14},{14,16},{16,18},{18... | collective-permute-start | bytes 786440 | tf_op jit(solution)/shard_map/ppermute | solution.py:16
  21.3 0.0 collective-permute-done
  21.3 0.0 collective-permute-start.2
  21.4 5.8 %fusion.1 = (f32[2,4,512]{2,1,0:T(4,128)S(1)}, f32[2,512,512,4]{2,1,3,0:T(8,128)}) fusion(pred[512,512]{0,1:T(8,128)(4,1)S(1)} %get-tuple-element.243, bf16[512,2,128,1]{0,2,3,1:T(8,128)(2,1)} %bitcast.47, bf16[512,2,4,128]{3,0,2,1:T(8,128)(2,1)S(1)} %bitcast.206), kind=kOutput, calls=%fused_computation.9 | convolution fusion | flops 543158272 | bytes 9977856 | tf_op jit(solution)/shard_map/qhgd,khd->hgqk/dot_general | solution.py:52
  27.2 0.0 collective-permute-done.3
  27.2 0.8 copy.30
  28.1 4.1 %collective-permute-start.5 = (bf16[512,256]{1,0:T(8,128)(2,1)S(1)}, bf16[512,256]{1,0:T(8,128)(2,1)S(1)}, u32[]{:S(2)}, u32[]{:S(2)}) collective-permute-start(bf16[512,256]{1,0:T(8,128)(2,1)S(1)} %collective-permute-done.3), channel_id=1, source_target_pairs={{0,2},{2,4},{4,6},{6,8},{8,10},{10,12},{12,14},{14,16},{16,18},{18... | collective-permute-start | bytes 786440 | tf_op jit(solution)/shard_map/ppermute | solution.py:16
  32.2 0.0 collective-permute-done.2
  32.2 2.0 %collective-permute-start.4 = (bf16[512,256]{0,1:T(8,128)(2,1)S(1)}, bf16[512,256]{0,1:T(8,128)(2,1)S(1)}, u32[]{:S(2)}, u32[]{:S(2)}) collective-permute-start(bf16[512,256]{0,1:T(8,128)(2,1)S(1)} %collective-permute-done.2), channel_id=1, source_target_pairs={{0,2},{2,4},{4,6},{6,8},{8,10},{10,12},{12,14},{14,16},{16,18},{18... | collective-permute-start | bytes 786440 | tf_op jit(solution)/shard_map/ppermute | solution.py:16
  34.2 0.0 slice-start
  34.2 2.0 %fusion.2 = (f32[2,4,512]{2,1,0:T(4,128)S(1)}, f32[2,512,512,4]{2,1,3,0:T(8,128)S(1)}) fusion(pred[512,512]{0,1:T(8,128)(4,1)S(1)} %get-tuple-element.244, bf16[512,2,128,1]{0,2,3,1:T(8,128)(2,1)S(1)} %bitcast.213, bf16[512,2,4,128]{3,0,2,1:T(8,128)(2,1)S(1)} %bitcast.207), kind=kOutput, calls=%fused_computation.10 | convolution fusion | flops 543158272 | bytes 9977856 | tf_op jit(solution)/shard_map/qhgd,khd->hgqk/dot_general | solution.py:52
  36.2 2.1 %collective-permute-done.4 = bf16[512,256]{0,1:T(8,128)(2,1)S(1)} collective-permute-done((bf16[512,256]{0,1:T(8,128)(2,1)S(1)}, bf16[512,256]{0,1:T(8,128)(2,1)S(1)}, u32[]{:S(2)}, u32[]{:S(2)}) %collective-permute-start.4) | collective-permute-done | bytes 262176 | tf_op jit(solution)/shard_map/ppermute | solution.py:16
  38.3 0.0 slice-start.1
  38.3 2.0 %fusion.3 = (f32[2,4,512]{2,1,0:T(4,128)S(1)}, f32[2,512,512,4]{2,1,3,0:T(8,128)S(1)}) fusion(pred[512,512]{0,1:T(8,128)(4,1)S(1)} %get-tuple-element.245, bf16[512,2,128,1]{0,2,3,1:T(8,128)(2,1)S(1)} %bitcast.214, bf16[512,2,4,128]{3,0,2,1:T(8,128)(2,1)S(1)} %bitcast.208), kind=kOutput, calls=%fused_computation.11 | convolution fusion | flops 543158272 | bytes 9977856 | tf_op jit(solution)/shard_map/qhgd,khd->hgqk/dot_general | solution.py:52
  40.4 0.0 copy-start
  40.4 0.0 slice-done
  40.4 0.1 slice-done.1
  40.5 2.0 %fusion.4 = f32[2,4,512]{2,1,0:T(4,128)S(1)} fusion(f32[2,512,512,4]{2,1,3,0:T(8,128)S(1)} %bitcast.202, f32[2,4,512]{2,1,0:T(4,128)S(1)} %get-tuple-element.241, pred[512,512]{0,1:T(8,128)(4,1)S(1)} %get-tuple-element.242), kind=kLoop, calls=%fused_computation.12 | loop fusion | flops 10481664 | bytes 8683520 | tf_op jit(solution)/shard_map/reduce_sum | solution.py:62
  42.5 0.0 slice-start.2
  42.6 0.0 slice-start.3
  42.6 3.8 %fusion.18 = f32[2,4,512,128]{2,3,1,0:T(8,128)} fusion(bf16[512,2,128,1]{0,2,3,1:T(8,128)(2,1)S(1)} %bitcast.216, f32[2,512,512,4]{2,1,3,0:T(8,128)S(1)} %bitcast.202, f32[2,4,512]{2,1,0:T(4,128)S(1)} %get-tuple-element.241, pred[512,512]{0,1:T(8,128)(4,1)S(1)} %get-tuple-element.242), kind=kOutput, calls=%fused_computation.23 | convolution fusion | flops 547356672 | bytes 11026432 | tf_op jit(solution)/shard_map/hgqk,khd->qhgd/dot_general | solution.py:63
  46.4 0.0 copy-start.2
  46.4 0.0 slice-done.2
  46.4 1.0 slice-done.3
  47.4 2.0 %fusion.6 = f32[2,4,512]{2,1,0:T(4,128)S(1)} fusion(f32[2,512,512,4]{2,1,3,0:T(8,128)S(1)} %bitcast.204, f32[2,4,512]{2,1,0:T(4,128)S(1)} %get-tuple-element.230, pred[512,512]{0,1:T(8,128)(4,1)S(1)} %get-tuple-element.243), kind=kLoop, calls=%fused_computation.14 | loop fusion | flops 10481664 | bytes 8683520 | tf_op jit(solution)/shard_map/reduce_sum | solution.py:62
  49.4 0.0 copy-done.2
  49.5 3.9 %fusion.16 = f32[2,4,512,128]{2,3,1,0:T(8,128)} fusion(bf16[512,2,128,1]{0,2,3,1:T(8,128)(2,1)S(1)} %bitcast.217, f32[2,512,512,4]{2,1,3,0:T(8,128)S(1)} %bitcast.204, f32[2,4,512]{2,1,0:T(4,128)S(1)} %get-tuple-element.230, pred[512,512]{0,1:T(8,128)(4,1)S(1)} %get-tuple-element.243), kind=kOutput, calls=%fused_computation.22 | convolution fusion | flops 547356672 | bytes 11026432 | tf_op jit(solution)/shard_map/hgqk,khd->qhgd/dot_general | solution.py:63
  53.3 0.0 copy-start.3
  53.3 2.0 %fusion.8 = f32[2,4,512]{2,1,0:T(4,128)S(1)} fusion(f32[2,512,512,4]{2,1,3,0:T(8,128)S(1)} %get-tuple-element.253, f32[2,4,512]{2,1,0:T(4,128)S(1)} %get-tuple-element.229, pred[512,512]{0,1:T(8,128)(4,1)S(1)} %get-tuple-element.244), kind=kLoop, calls=%fused_computation.16 | loop fusion | flops 10481664 | bytes 8683520 | tf_op jit(solution)/shard_map/reduce_sum | solution.py:62
  55.3 0.0 copy-done.3
  55.4 3.8 %fusion.14 = f32[2,4,512,128]{2,3,1,0:T(8,128)} fusion(bf16[512,2,128,1]{0,2,3,1:T(8,128)(2,1)S(1)} %bitcast.218, f32[2,512,512,4]{2,1,3,0:T(8,128)S(1)} %get-tuple-element.253, f32[2,4,512]{2,1,0:T(4,128)S(1)} %get-tuple-element.229, pred[512,512]{0,1:T(8,128)(4,1)S(1)} %get-tuple-element.244), kind=kOutput, calls=%fused_computation.21 | convolution fusion | flops 547356672 | bytes 11026432 | tf_op jit(solution)/shard_map/hgqk,khd->qhgd/dot_general | solution.py:63
  59.2 0.0 copy-done
  59.2 2.0 %fusion.10 = f32[2,4,512]{2,1,0:T(4,128)S(1)} fusion(f32[2,512,512,4]{2,1,3,0:T(8,128)S(1)} %get-tuple-element.251, f32[2,4,512]{2,1,0:T(4,128)S(1)} %get-tuple-element.228, pred[512,512]{0,1:T(8,128)(4,1)S(1)} %get-tuple-element.245), kind=kLoop, calls=%fused_computation.18 | loop fusion | flops 10481664 | bytes 8683520 | tf_op jit(solution)/shard_map/reduce_sum | solution.py:62
  61.2 0.0 collective-permute-done.5
  61.3 0.1 copy.33
  61.4 8.1 %fusion.25 = bf16[512,2,4,128]{0,3,2,1:T(8,128)(2,1)S(1)} fusion(f32[2,4,512,128]{2,3,1,0:T(8,128)} %fusion.14, f32[2,4,512,128]{2,3,1,0:T(8,128)} %fusion.16, f32[2,4,512,128]{2,3,1,0:T(8,128)} %fusion.18, bf16[512,2,128,1]{0,2,3,1:T(8,128)(2,1)S(1)} %bitcast.219, f32[2,512,512,4]{2,1,3,0:T(8,128)} %copy-done, f32[2,4,512]{2,1,0:T(4,128)S(1)} %get-tuple-element.228, ...), kind=kOutput, calls=%fused_computation.32 | convolution fusion | flops 552075264 | bytes 16351232 | tf_op jit(solution)/shard_map/hgqk,khd->qhgd/dot_general | solution.py:63
  69.5 0.2 pad_maximum_fusion
  69.7 29.3 %all_to_all.5 = bf16[2,512,1024]{1,2,0:T(8,128)(2,1)S(1)} all-to-all(bf16[2,512,1024]{1,2,0:T(8,128)(2,1)S(1)} %pad_maximum_fusion), channel_id=1, replica_groups=mesh['ctx'=128,'head'=2] {'head'}, dimensions={0} | all-to-all | bytes 4194304 | tf_op jit(solution)/shard_map/all_to_all | solution.py:132
  99.0 9.1 %convolution_convert_fusion = bf16[512,2048]{1,0:T(8,128)(2,1)} fusion(bf16[512,2048]{0,1:T(8,128)(2,1)S(1)} %bitcast.211, bf16[2048,2048]{1,0:T(8,128)(2,1)} %param.55), kind=kOutput, calls=%fused_computation.28 | convolution fusion | flops 4296015872 | bytes 12582912 | tf_op jit(solution)/shard_map/dot_general | solution.py:130
  (6 shorter events, 0.1 us)
Async XLA Ops:
  0.0 8.9 %copy-start.1 = (bf16[512,1024]{1,0:T(8,128)(2,1)S(1)}, bf16[512,1024]{1,0:T(8,128)(2,1)}, u32[]{:S(2)}) copy-start(bf16[512,1024]{1,0:T(8,128)(2,1)} %param.51) | copy-start | bytes 3145732
  4.5 16.8 %collective-permute-start = (bf16[512,256]{0,1:T(8,128)(2,1)S(1)}, bf16[512,256]{0,1:T(8,128)(2,1)}, u32[]{:S(2)}, u32[]{:S(2)}) collective-permute-start(bf16[512,256]{0,1:T(8,128)(2,1)S(1)} %bitcast.215), channel_id=1, source_target_pairs={{0,2},{2,4},{4,6},{6,8},{8,10},{10,12},{12,14},{14,16},{16,18},{18... | collective-permute-start | bytes 786440 | tf_op jit(solution)/shard_map/ppermute | solution.py:16
  7.6 9.8 %collective-permute-start.1 = (bf16[512,256]{1,0:T(8,128)(2,1)}, bf16[512,256]{1,0:T(8,128)(2,1)S(1)}, u32[]{:S(2)}, u32[]{:S(2)}) collective-permute-start(bf16[512,256]{1,0:T(8,128)(2,1)} %param.53), channel_id=1, source_target_pairs={{0,2},{2,4},{4,6},{6,8},{8,10},{10,12},{12,14},{14,16},{16,18},{18... | collective-permute-start | bytes 786440 | tf_op jit(solution)/shard_map/ppermute | solution.py:16
  18.3 8.9 %collective-permute-start.3 = (bf16[512,256]{1,0:T(8,128)(2,1)S(1)}, bf16[512,256]{1,0:T(8,128)(2,1)S(1)}, u32[]{:S(2)}, u32[]{:S(2)}) collective-permute-start(bf16[512,256]{1,0:T(8,128)(2,1)S(1)} %collective-permute-done.1), channel_id=1, source_target_pairs={{0,2},{2,4},{4,6},{6,8},{8,10},{10,12},{12,14},{14,16},{16,18},{18... | collective-permute-start | bytes 786440 | tf_op jit(solution)/shard_map/ppermute | solution.py:16
  21.3 10.9 %collective-permute-start.2 = (bf16[512,256]{0,1:T(8,128)(2,1)}, bf16[512,256]{0,1:T(8,128)(2,1)S(1)}, u32[]{:S(2)}, u32[]{:S(2)}) collective-permute-start(bf16[512,256]{0,1:T(8,128)(2,1)} %collective-permute-done), channel_id=1, source_target_pairs={{0,2},{2,4},{4,6},{6,8},{8,10},{10,12},{12,14},{14,16},{16,18},{18... | collective-permute-start | bytes 786440 | tf_op jit(solution)/shard_map/ppermute | solution.py:16
  28.1 33.2 %collective-permute-start.5 = (bf16[512,256]{1,0:T(8,128)(2,1)S(1)}, bf16[512,256]{1,0:T(8,128)(2,1)S(1)}, u32[]{:S(2)}, u32[]{:S(2)}) collective-permute-start(bf16[512,256]{1,0:T(8,128)(2,1)S(1)} %collective-permute-done.3), channel_id=1, source_target_pairs={{0,2},{2,4},{4,6},{6,8},{8,10},{10,12},{12,14},{14,16},{16,18},{18... | collective-permute-start | bytes 786440 | tf_op jit(solution)/shard_map/ppermute | solution.py:16
  32.2 6.1 %collective-permute-start.4 = (bf16[512,256]{0,1:T(8,128)(2,1)S(1)}, bf16[512,256]{0,1:T(8,128)(2,1)S(1)}, u32[]{:S(2)}, u32[]{:S(2)}) collective-permute-start(bf16[512,256]{0,1:T(8,128)(2,1)S(1)} %collective-permute-done.2), channel_id=1, source_target_pairs={{0,2},{2,4},{4,6},{6,8},{8,10},{10,12},{12,14},{14,16},{16,18},{18... | collective-permute-start | bytes 786440 | tf_op jit(solution)/shard_map/ppermute | solution.py:16
  34.2 6.2 %slice-start = ((s8[8388608]{0:T(1024)(128)(4,1)}), s8[4194304]{0:T(1024)(128)(4,1)S(1)}, s32[]{:S(2)}) async-start(s8[8388608]{0:T(1024)(128)(4,1)} %bitcast.201), calls=%async_computation.1 | async-start | bytes 8388608
  38.3 2.2 %slice-start.1 = ((s8[8388608]{0:T(1024)(128)(4,1)}), s8[4194304]{0:T(1024)(128)(4,1)S(1)}, s32[]{:S(2)}) async-start(s8[8388608]{0:T(1024)(128)(4,1)} %bitcast.201), calls=%async_computation.2 | async-start | bytes 8388608
  40.4 18.8 %copy-start = (f32[2,512,512,4]{2,1,3,0:T(8,128)}, f32[2,512,512,4]{2,1,3,0:T(8,128)S(1)}, u32[]{:S(2)}) copy-start(f32[2,512,512,4]{2,1,3,0:T(8,128)S(1)} %get-tuple-element.251) | copy-start | bytes 25165828
  42.5 3.9 %slice-start.2 = ((s8[8388608]{0:T(1024)(128)(4,1)}), s8[4194304]{0:T(1024)(128)(4,1)S(1)}, s32[]{:S(2)}) async-start(s8[8388608]{0:T(1024)(128)(4,1)} %bitcast.203), calls=%async_computation.3 | async-start | bytes 8388608
  42.6 4.9 %slice-start.3 = ((s8[8388608]{0:T(1024)(128)(4,1)}), s8[4194304]{0:T(1024)(128)(4,1)S(1)}, s32[]{:S(2)}) async-start(s8[8388608]{0:T(1024)(128)(4,1)} %bitcast.203), calls=%async_computation.4 | async-start | bytes 8388608
  46.4 3.1 %copy-start.2 = (bf16[512,256]{0,1:T(8,128)(2,1)S(1)}, bf16[512,256]{0,1:T(8,128)(2,1)}, u32[]{:S(2)}) copy-start(bf16[512,256]{0,1:T(8,128)(2,1)} %copy.27) | copy-start | bytes 786436
  53.3 2.0 %copy-start.3 = (bf16[512,256]{0,1:T(8,128)(2,1)S(1)}, bf16[512,256]{0,1:T(8,128)(2,1)}, u32[]{:S(2)}) copy-start(bf16[512,256]{0,1:T(8,128)(2,1)} %copy.30) | copy-start | bytes 786436
